TPU v7x, 32 devices: a whole 2x2x4 slice. The times are simulated.
32 devices in a mesh: dp: 8 (over z, x), seq: 4 (over y, core).
Axes of the slice: x: 2, y: 2, z: 4, core: 2. Of those that a mesh axis runs over, the one named last changes fastest.
Arguments:
- tokens: bfloat16 [16384, 1024], P(('dp', 'seq')), may hold values from -6 to 6
- out_grad: bfloat16 [16384, 1024], P(('dp', 'seq')), may hold values from -6 to 6
- qkv_weight: bfloat16 [1024, 3072], P('dp'), may hold values from -0.25 to 0.25
- qv_bias: bfloat16 [2, 1024], P(None, 'dp'), may hold values from -3 to 3
- proj_weight: bfloat16 [1024, 1024], P('dp'), may hold values from -0.1875 to 0.1875
- fc1_weight: bfloat16 [1024, 4096], P('dp'), may hold values from -0.1875 to 0.1875
- fc1_bias: bfloat16 [4096], P('dp'), may hold values from -3 to 3
- fc2_weight: bfloat16 [4096, 1024], P('dp'), may hold values from -0.09375 to 0.09375
- out_bias: bfloat16 [2, 1024], P(None, 'dp'), may hold values from -3 to 3
- norm_gains: bfloat16 [4, 1024], P(None, 'dp'), may hold values from 0.5 to 1.5
- norm_shifts: bfloat16 [4, 1024], P(None, 'dp'), may hold values from -2 to 2
Outputs:
- layer_out: bfloat16 [16384, 1024], P(('dp', 'seq'))
- tokens_grad: bfloat16 [16384, 1024], P(('dp', 'seq'))
- qkv_weight_grad: float32 [1024, 3072], P('dp')
- qv_bias_grad: float32 [2, 1024], P(None, 'dp')
- proj_weight_grad: float32 [1024, 1024], P('dp')
- fc1_weight_grad: float32 [1024, 4096], P('dp')
- fc1_bias_grad: float32 [4096], P('dp')
- fc2_weight_grad: float32 [4096, 1024], P('dp')
- out_bias_grad: float32 [2, 1024], P(None, 'dp')
- norm_gains_grad: float32 [4, 1024], P(None, 'dp')
- norm_shifts_grad: float32 [4, 1024], P(None, 'dp')
All inputs are finite; a program needn't handle non-finite values.
Results may differ from a plain program's by a relative error of at most 0.015.
The roundings to bfloat16 on the way count: a program that leaves them out, or rounds other values in their place, can miss the bound.
Values may be sent and summed in bfloat16 or wider, within the bound.
No kernel may reach another device: no remote copies, remote signals or barrier semaphores. Data moves between devices by JAX's collectives and lax.ppermute only.
A program may use at most 192 MiB of HBM per device.

v0:
```python
from functools import partial
import math
import jax
import jax.numpy as jnp
from jax import lax
from jax.sharding import PartitionSpec as P

HEAD_DIM = 64
RELAX_ALPHA = 32.0
NORM_EPS = 1e-05


def layer_norm(values, gain_vec, shift_vec):
    centred = values - jnp.mean(values, axis=-1, keepdims=True)
    variance = jnp.mean(centred * centred, axis=-1, keepdims=True)
    return centred * lax.rsqrt(variance + NORM_EPS) * gain_vec + shift_vec


def contract_rows(left, right):
    return lax.dot_general(
        left, right, (((0,), (0,)), ((), ())), preferred_element_type=jnp.float32
    )


def contract_cols(left, right):
    return lax.dot_general(
        left, right, (((1,), (1,)), ((), ())), preferred_element_type=jnp.float32
    )


def norm_backward(values, gain_vec, shift_vec, upstream):
    unused_out, pullback = jax.vjp(layer_norm, values, gain_vec, shift_vec)
    return pullback(upstream)


def column_sums(values):
    return jnp.sum(values.astype(jnp.float32), axis=0)


def causal_logits(scores, block_start):
    row_index = block_start + lax.iota(jnp.int32, scores.shape[0])
    col_index = lax.iota(jnp.int32, scores.shape[1])
    return jnp.where(row_index[:, None] >= col_index[None, :], RELAX_ALPHA * scores, -1e30)


def block_layout(seq_len):
    block_rows = min(512, seq_len)
    return (block_rows, seq_len // block_rows)


def head_column(array, head_index):
    return lax.dynamic_index_in_dim(array, head_index, axis=1, keepdims=False)


def head_block(array, head_index, block_start, block_rows):
    piece = lax.dynamic_slice(
        array, (block_start, head_index, jnp.int32(0)), (block_rows, 1, array.shape[2])
    )
    return piece.reshape(block_rows, array.shape[2])


def scale_table():
    query_scale = 1.0 / (RELAX_ALPHA * math.sqrt(HEAD_DIM))
    return jnp.array([query_scale, 1.0, 1.0], jnp.float32)[:, None]


def gather_attention(qkv_weight, qv_bias, proj_weight, out_bias, norm_gains, norm_shifts):
    return (
        lax.all_gather(qkv_weight, "dp", axis=0, tiled=True),
        lax.all_gather(qv_bias, "dp", axis=1, tiled=True),
        lax.all_gather(proj_weight, "dp", axis=0, tiled=True),
        lax.all_gather(out_bias, "dp", axis=1, tiled=True),
        lax.all_gather(norm_gains, "dp", axis=1, tiled=True),
        lax.all_gather(norm_shifts, "dp", axis=1, tiled=True),
    )


def gather_mlp(fc1_weight, fc1_bias, fc2_weight):
    return (
        lax.all_gather(fc1_weight, "dp", axis=0, tiled=True),
        lax.all_gather(fc1_bias, "dp", axis=0, tiled=True),
        lax.all_gather(fc2_weight, "dp", axis=0, tiled=True),
    )


def run_forward(tokens, attn_full, mlp_full):
    qkv_w, qv_b, proj_w, out_b, gains_low, shifts_low = attn_full
    fc1_w, fc1_b, fc2_w = mlp_full
    gain_rows = gains_low.astype(jnp.float32)
    shift_rows = shifts_low.astype(jnp.float32)
    model_width = qkv_w.shape[0]
    tok_rows = tokens.shape[0]
    tok_vals = tokens.astype(jnp.float32)
    normed = layer_norm(tok_vals, gain_rows[0], shift_rows[0]).astype(jnp.bfloat16)
    mixed_cols = jnp.dot(normed, qkv_w, preferred_element_type=jnp.float32).reshape(
        tok_rows, 3, model_width
    )
    bias_rows = qv_b.astype(jnp.float32)
    bias_three = jnp.stack((bias_rows[0], jnp.zeros_like(bias_rows[0]), bias_rows[1]))
    stacked = ((mixed_cols + bias_three) * scale_table()).astype(jnp.bfloat16)
    by_heads = lax.all_to_all(stacked, "seq", split_axis=2, concat_axis=0, tiled=True)
    seq_len = by_heads.shape[0]
    local_heads = by_heads.shape[2] // HEAD_DIM
    head_split = by_heads.reshape(seq_len, 3, local_heads, HEAD_DIM)
    queries = head_split[:, 0]
    key_rows = head_split[:, 1]
    values = head_split[:, 2]
    block_rows, blocks = block_layout(seq_len)

    def one_block(step_index):
        head_index = step_index // blocks
        block_start = step_index % blocks * block_rows
        q_block = head_block(queries, head_index, block_start, block_rows)
        k_head = head_column(key_rows, head_index)
        v_head = head_column(values, head_index)
        scores = contract_cols(q_block, k_head)
        logits = causal_logits(scores, block_start)
        row_top = jnp.max(logits, axis=-1, keepdims=True)
        powers = jnp.exp(logits - row_top)
        row_total = jnp.sum(powers, axis=-1, keepdims=True)
        probs_low = (powers / row_total).astype(jnp.bfloat16)
        out_block = jnp.dot(probs_low, v_head, preferred_element_type=jnp.float32)
        return (out_block.astype(jnp.bfloat16), (row_top + jnp.log(row_total))[:, 0])

    out_blocks, lse_blocks = lax.map(one_block, lax.iota(jnp.int32, local_heads * blocks))
    attended_heads = (
        out_blocks.reshape(local_heads, seq_len, HEAD_DIM)
        .transpose(1, 0, 2)
        .reshape(seq_len, local_heads * HEAD_DIM)
    )
    attended = lax.all_to_all(attended_heads, "seq", split_axis=0, concat_axis=1, tiled=True)
    branch = jnp.dot(attended, proj_w, preferred_element_type=jnp.float32) + out_b[0].astype(
        jnp.float32
    )
    residual = tok_vals + layer_norm(branch, gain_rows[1], shift_rows[1])
    normed_two = layer_norm(residual, gain_rows[2], shift_rows[2]).astype(jnp.bfloat16)
    hidden = jnp.dot(normed_two, fc1_w, preferred_element_type=jnp.float32) + fc1_b.astype(
        jnp.float32
    )
    active = jax.nn.gelu(hidden, approximate=True).astype(jnp.bfloat16)
    second = jnp.dot(active, fc2_w, preferred_element_type=jnp.float32) + out_b[1].astype(
        jnp.float32
    )
    layer_out = residual + layer_norm(second, gain_rows[3], shift_rows[3])
    kept_state = (
        tok_vals,
        normed,
        queries,
        key_rows,
        values,
        lse_blocks,
        attended,
        branch,
        residual,
        normed_two,
        hidden,
        active,
        second,
    )
    return (layer_out, kept_state)


def per_device(
    tokens,
    out_grad,
    qkv_weight,
    qv_bias,
    proj_weight,
    fc1_weight,
    fc1_bias,
    fc2_weight,
    out_bias,
    norm_gains,
    norm_shifts,
):
    attn_full = gather_attention(
        qkv_weight, qv_bias, proj_weight, out_bias, norm_gains, norm_shifts
    )
    mlp_full = gather_mlp(fc1_weight, fc1_bias, fc2_weight)
    layer_out, kept_state = run_forward(tokens, attn_full, mlp_full)
    attn_full = gather_attention(
        qkv_weight, qv_bias, proj_weight, out_bias, norm_gains, norm_shifts
    )
    mlp_full = gather_mlp(fc1_weight, fc1_bias, fc2_weight)
    repeat_out, kept_state = run_forward(tokens, attn_full, mlp_full)
    qkv_w, qv_b, proj_w, out_b, gains_low, shifts_low = attn_full
    fc1_w, fc1_b, fc2_w = mlp_full
    gain_rows = gains_low.astype(jnp.float32)
    shift_rows = shifts_low.astype(jnp.float32)
    (
        tok_vals,
        normed,
        queries,
        key_rows,
        values,
        lse_blocks,
        attended,
        branch,
        residual,
        normed_two,
        hidden,
        active,
        second,
    ) = kept_state
    tok_rows = tok_vals.shape[0]
    model_width = qkv_w.shape[0]
    upstream = out_grad.astype(jnp.float32)
    d_second, grad_gain_three, grad_shift_three = norm_backward(
        second, gain_rows[3], shift_rows[3], upstream
    )
    d_second = d_second.astype(jnp.bfloat16)
    grad_fc2 = contract_rows(active, d_second)
    grad_bias_two = column_sums(d_second)
    d_active = contract_cols(d_second, fc2_w)
    unused_gelu, gelu_back = jax.vjp(partial(jax.nn.gelu, approximate=True), hidden)
    d_hidden = gelu_back(d_active)[0].astype(jnp.bfloat16)
    grad_fc1 = contract_rows(normed_two, d_hidden)
    grad_fc1_bias = column_sums(d_hidden)
    d_normed_two = contract_cols(d_hidden, fc1_w)
    d_resid_part, grad_gain_two, grad_shift_two = norm_backward(
        residual, gain_rows[2], shift_rows[2], d_normed_two
    )
    d_residual = upstream + d_resid_part
    d_branch, grad_gain_one, grad_shift_one = norm_backward(
        branch, gain_rows[1], shift_rows[1], d_residual
    )
    d_branch = d_branch.astype(jnp.bfloat16)
    grad_proj = contract_rows(attended, d_branch)
    grad_bias_one = column_sums(d_branch)
    d_attended = contract_cols(d_branch, proj_w).astype(jnp.bfloat16)
    seq_len = queries.shape[0]
    local_heads = queries.shape[1]
    block_rows, blocks = block_layout(seq_len)
    d_heads = lax.all_to_all(d_attended, "seq", split_axis=1, concat_axis=0, tiled=True).reshape(
        seq_len, local_heads, HEAD_DIM
    )
    zero_grad = jnp.zeros(queries.shape, jnp.float32)

    def back_step(grad_pair, step_index):
        key_grad, value_grad = grad_pair
        head_index = step_index // blocks
        block_start = step_index % blocks * block_rows
        q_block = head_block(queries, head_index, block_start, block_rows)
        d_block = head_block(d_heads, head_index, block_start, block_rows)
        k_head = head_column(key_rows, head_index)
        v_head = head_column(values, head_index)
        scores = contract_cols(q_block, k_head)
        probs = jnp.exp(causal_logits(scores, block_start) - lse_blocks[step_index][:, None])
        d_probs = contract_cols(d_block, v_head)
        row_delta = jnp.sum(probs * d_probs, axis=-1, keepdims=True)
        d_scores = (RELAX_ALPHA * probs * (d_probs - row_delta)).astype(jnp.bfloat16)
        query_grad = jnp.dot(d_scores, k_head, preferred_element_type=jnp.float32)
        key_add = contract_rows(d_scores, q_block)
        value_add = contract_rows(probs.astype(jnp.bfloat16), d_block)
        key_grad = lax.dynamic_update_index_in_dim(
            key_grad, head_column(key_grad, head_index) + key_add, head_index, 1
        )
        value_grad = lax.dynamic_update_index_in_dim(
            value_grad, head_column(value_grad, head_index) + value_add, head_index, 1
        )
        return ((key_grad, value_grad), query_grad.astype(jnp.bfloat16))

    (key_grad, value_grad), query_blocks = lax.scan(
        back_step, (zero_grad, zero_grad), lax.iota(jnp.int32, local_heads * blocks)
    )
    query_grad = query_blocks.reshape(local_heads, seq_len, HEAD_DIM).transpose(1, 0, 2)
    back_stack = jnp.stack(
        (query_grad, key_grad.astype(jnp.bfloat16), value_grad.astype(jnp.bfloat16)), axis=1
    ).reshape(seq_len, 3, local_heads * HEAD_DIM)
    back_tokens = lax.all_to_all(back_stack, "seq", split_axis=0, concat_axis=2, tiled=True)
    d_mixed = (
        (back_tokens.astype(jnp.float32) * scale_table())
        .astype(jnp.bfloat16)
        .reshape(tok_rows, 3 * model_width)
    )
    grad_qkv = contract_rows(normed, d_mixed)
    mixed_sums = column_sums(d_mixed).reshape(3, model_width)
    grad_qv_bias = jnp.stack((mixed_sums[0], mixed_sums[2]))
    d_normed = contract_cols(d_mixed, qkv_w)
    d_tok_part, grad_gain_zero, grad_shift_zero = norm_backward(
        tok_vals, gain_rows[0], shift_rows[0], d_normed
    )
    tokens_grad = (d_residual + d_tok_part).astype(jnp.bfloat16)
    grad_out_bias = jnp.stack((grad_bias_one, grad_bias_two))
    grad_gains = jnp.stack((grad_gain_zero, grad_gain_one, grad_gain_two, grad_gain_three))
    grad_shifts = jnp.stack((grad_shift_zero, grad_shift_one, grad_shift_two, grad_shift_three))
    owned = (
        lax.psum_scatter(grad_qkv, "dp", scatter_dimension=0, tiled=True),
        lax.psum_scatter(grad_qv_bias, "dp", scatter_dimension=1, tiled=True),
        lax.psum_scatter(grad_proj, "dp", scatter_dimension=0, tiled=True),
        lax.psum_scatter(grad_fc1, "dp", scatter_dimension=0, tiled=True),
        lax.psum_scatter(grad_fc1_bias, "dp", scatter_dimension=0, tiled=True),
        lax.psum_scatter(grad_fc2, "dp", scatter_dimension=0, tiled=True),
        lax.psum_scatter(grad_out_bias, "dp", scatter_dimension=1, tiled=True),
        lax.psum_scatter(grad_gains, "dp", scatter_dimension=1, tiled=True),
        lax.psum_scatter(grad_shifts, "dp", scatter_dimension=1, tiled=True),
    )
    totals = (
        lax.psum(owned[0].astype(jnp.bfloat16), "seq").astype(jnp.float32),
        lax.psum(owned[1].astype(jnp.bfloat16), "seq").astype(jnp.float32),
        lax.psum(owned[2].astype(jnp.bfloat16), "seq").astype(jnp.float32),
        lax.psum(owned[3].astype(jnp.bfloat16), "seq").astype(jnp.float32),
        lax.psum(owned[4].astype(jnp.bfloat16), "seq").astype(jnp.float32),
        lax.psum(owned[5].astype(jnp.bfloat16), "seq").astype(jnp.float32),
        lax.psum(owned[6].astype(jnp.bfloat16), "seq").astype(jnp.float32),
        lax.psum(owned[7].astype(jnp.bfloat16), "seq").astype(jnp.float32),
        lax.psum(owned[8].astype(jnp.bfloat16), "seq").astype(jnp.float32),
    )
    return (
        layer_out.astype(jnp.bfloat16),
        tokens_grad,
        totals[0],
        totals[1],
        totals[2],
        totals[3],
        totals[4],
        totals[5],
        totals[6],
        totals[7],
        totals[8],
    )


def solution(mesh):
    placed = (
        P(("dp", "seq"), None),
        P(("dp", "seq"), None),
        P("dp", None),
        P(None, "dp"),
        P("dp", None),
        P("dp", None),
        P("dp"),
        P("dp", None),
        P(None, "dp"),
        P(None, "dp"),
        P(None, "dp"),
    )
    return jax.shard_map(
        per_device,
        mesh=mesh,
        in_specs=placed,
        out_specs=(
            P(("dp", "seq"), None),
            P(("dp", "seq"), None),
            P("dp", None),
            P(None, "dp"),
            P("dp", None),
            P("dp", None),
            P("dp"),
            P("dp", None),
            P(None, "dp"),
            P(None, "dp"),
            P(None, "dp"),
        ),
        check_vma=False,
    )
```

profile of v0, /device:TPU:0, one launch (start us, length us, event | category | flops | bytes accessed | tf_op | source)
XLA Modules:
  0.0 2192.8 jit_solution(13262523268789830104)
XLA Ops:
  9.5 22.3 %all_gather.39 = bf16[2,1024]{1,0:T(2,128)(2,1)S(1)} all-gather(bf16[2,128]{1,0:T(2,128)(2,1)S(1)} %copy-done.48), channel_id=1, replica_groups=mesh['dp'=8,'seq'=4] {'dp'}, dimensions={1}, use_global_device_ids=true | all-gather | bytes 4608 | tf_op jit(solution)/shard_map/all_gather | solution.py:70
  31.8 16.7 all_gather.36
  48.5 18.3 all_gather.37
  69.3 42.9 %all-gather.6.cloned.1.call-done = bf16[1024,3072]{1,0:T(8,128)(2,1)} async-done(((bf16[128,3072]{1,0:T(8,128)(2,1)}), bf16[1024,3072]{1,0:T(8,128)(2,1)}) %all-gather.6.cloned.1.call-update) | async-done | bytes 6291472 | tf_op jit(solution)/shard_map/all_gather | solution.py:69
  129.0 47.6 %all-to-all-done = bf16[512,3,1024]{0,1,2:T(4,128)(2,1)} async-done(((bf16[512,3,1024]{0,1,2:T(4,128)(2,1)}), bf16[512,3,1024]{0,1,2:T(4,128)(2,1)}, u32[]{:S(2)}, u32[]{:S(2)}) %all-to-all-start) | async-done | bytes 3145760 | tf_op jit(solution)/shard_map/all_to_all | solution.py:101
  183.7 6.1 reshape.336
  194.1 119.5 %while.42 = (s32[]{:T(128)}, bf16[16,512,64]{1,2,0:T(8,128)(2,1)}, s32[16]{0:T(128)S(1)}, bf16[2048,4,64]{0,2,1:T(8,128)(2,1)}, bf16[2048,4,64]{0,2,1:T(8,128)(2...) while((s32[]{:T(128)}, bf16[16,512,64]{1,2,0:T(8,128)(2,1)}, ...), condition=%wide.region_5.6_spmd, body=%wide.region_2.5_spmd.sunk | while | flops 277904928 | bytes 13255076 | solution.py:125
  332.3 174.0 %while.43 = (s32[]{:T(128)}, bf16[16,512,64]{1,2,0:T(8,128)(2,1)}, f32[16,512]{1,0:T(8,128)S(1)}, s32[16]{0:T(128)S(1)}, bf16[2048,4,64]{0,2,1:T(8,128)(2,1)}, /...) while((s32[]{:T(128)}, bf16[16,512,64]{1,2,0:T(8,128)(2,1)}, ...), condition=%wide.region_15.16_spmd, body=%wide.region_12.15_spmd.sunk | while | flops 277905440 | bytes 30042572 | solution.py:125
  519.7 26.0 %all-gather = bf16[8,1,512]{2,1,0:T(2,128)(2,1)S(1)} all-gather(bf16[1,1,512]{2,1,0:T(2,128)(2,1)S(1)} %reshape.355), channel_id=1, replica_groups=mesh['dp'=8,'seq'=4] {'dp'}, dimensions={0}, use_global_device_ids=true | all-gather | bytes 9216 | tf_op jit(solution)/shard_map/all_gather | solution.py:81
  545.7 16.2 all_gather.41
  576.5 11.9 fusion.99
  588.5 12.5 add_reduce_fusion
  601.0 18.2 multiply_reduce_fusion.5
  627.8 16.6 convert_reduce_fusion
  644.4 7.0 multiply_reduce_fusion.1
  666.3 10.5 all-to-all-done.3
  682.2 300.8 %while.44 = (s32[]{:T(128)}, f32[2048,4,64]{0,2,1:T(8,128)S(1)}, f32[2048,4,64]{0,2,1:T(8,128)}, bf16[16,512,64]{1,2,0:T(8,128)(2,1)}, s32[16]{0:T(128)S(1)}, /*...) while((s32[]{:T(128)}, f32[2048,4,64]{0,2,1:T(8,128)S(1)}, ...), condition=%wide.region_30.31_spmd, body=%wide.region_28.30_spmd.sunk | while | flops 682917888 | bytes 53564424 | solution.py:263
  1000.2 48.1 %all-to-all-done.4 = bf16[2048,3,256]{2,1,0:T(4,128)(2,1)} async-done(((bf16[2048,3,256]{2,1,0:T(4,128)(2,1)}), bf16[2048,3,256]{2,1,0:T(4,128)(2,1)}, u32[]{:S(2)}, u32[]{:S(2)}) %all-to-all-start.4) | async-done | bytes 3145760 | tf_op jit(solution)/shard_map/all_to_all | solution.py:270
  1054.2 6.6 copy.66
  1066.1 6.9 fusion.93
  1074.6 10.4 fusion.98
  1086.3 15.5 fusion.100
  1103.6 6.9 fusion.102
  1120.6 157.7 %reduce-scatter.17.cloned.1.call-done = f32[128,3072]{1,0:T(8,128)} async-done(((f32[1024,3072]{1,0:T(8,128)}), f32[128,3072]{1,0:T(8,128)}) %reduce-scatter.17.cloned.1.call-update) | async-done | bytes 1572880 | tf_op jit(solution)/shard_map/reduce_scatter | solution.py:288
  1280.7 283.0 %reduce-scatter.21.cloned.1.call-done = f32[128,4096]{1,0:T(8,128)} async-done(((f32[1024,4096]{1,0:T(8,128)}), f32[128,4096]{1,0:T(8,128)}) %reduce-scatter.21.cloned.1.call-update) | async-done | bytes 2097168 | tf_op jit(solution)/shard_map/reduce_scatter | solution.py:291
  1566.4 282.8 %reduce-scatter.23.cloned.1.call-done = f32[512,1024]{1,0:T(8,128)} async-done(((f32[4096,1024]{1,0:T(8,128)}), f32[512,1024]{1,0:T(8,128)}) %reduce-scatter.23.cloned.1.call-update) | async-done | bytes 2097168 | tf_op jit(solution)/shard_map/reduce_scatter | solution.py:293
  1853.8 35.3 %all-reduce = bf16[4096]{0:T(1024)(128)(2,1)S(1)} all-reduce(f32[4096]{0:T(1024)S(1)} %get-tuple-element.399), channel_id=6, replica_groups=mesh['dp'=8,'seq'=4] {'dp'}, use_global_device_ids=true, to_apply=%region_43.44.clone | all-reduce | flops 4096 | bytes 24576
  1889.2 25.3 %reduce-scatter.27.cloned.1.call-done = f32[128,2]{1,0:T(8,128)} async-done(((f32[1024,2]{1,0:T(8,128)}), f32[128,2]{1,0:T(8,128)}) %reduce-scatter.27.cloned.1.call-update) | async-done | bytes 1040
  1918.7 60.5 %reduce-scatter.25.cloned.1.call-done = f32[128,2]{1,0:T(8,128)} async-done(((f32[1024,2]{1,0:T(8,128)}), f32[128,2]{1,0:T(8,128)}) %reduce-scatter.25.cloned.1.call-update) | async-done | bytes 1040
  1980.1 63.8 %reduce-scatter.31.cloned.1.call-done = f32[128,4]{1,0:T(8,128)} async-done(((f32[1024,4]{1,0:T(8,128)}), f32[128,4]{1,0:T(8,128)}) %reduce-scatter.31.cloned.1.call-update) | async-done | bytes 2064
  2044.8 63.3 %reduce-scatter.29.cloned.1.call-done = f32[128,4]{1,0:T(8,128)} async-done(((f32[1024,4]{1,0:T(8,128)}), f32[128,4]{1,0:T(8,128)}) %reduce-scatter.29.cloned.1.call-update) | async-done | bytes 2064
  2117.5 62.0 %all-reduce.5.cloned.1.call-done = (bf16[128,3072]{1,0:T(8,128)(2,1)}, bf16[128,1024]{1,0:T(8,128)(2,1)}, bf16[128,4096]{1,0:T(8,128)(2,1)}, bf16[512,1024]{1,0:T(8,128)(2,1)}) async-done(((bf16[128,3072]{1,0:T(8,128)(2,1)}, bf16[128,1024]{1,0:T(8,128)(2,1)}, bf16[128,4096]{1,0:T(8,128)(2,1)}, bf16[512,1024]{1,0:T(8,128)(2,1)}), (bf16[128,3072]{1,0:T(8,128)(2,1)}, bf16[128,1024]{1,0:T(8,128)(2,1)}, ...) | async-done | bytes 3145744 | tf_op jit(solution)/shard_map/psum | solution.py:299
  (676 shorter events, 628.0 us)
Async XLA Ops:
  7.2 24.6 %copy-start.45 = (bf16[4,128]{1,0:T(4,128)(2,1)S(1)}, bf16[4,128]{1,0:T(4,128)(2,1)}, u32[]{:S(2)}) copy-start(bf16[4,128]{1,0:T(4,128)(2,1)} %param.29) | copy-start | bytes 3076
  7.2 41.3 %copy-start.46 = (bf16[4,128]{1,0:T(4,128)(2,1)S(1)}, bf16[4,128]{1,0:T(4,128)(2,1)}, u32[]{:S(2)}) copy-start(bf16[4,128]{1,0:T(4,128)(2,1)} %param.30) | copy-start | bytes 3076
  7.2 59.6 %copy-start.2 = (bf16[512,1024]{1,0:T(8,128)(2,1)S(1)}, bf16[512,1024]{1,0:T(8,128)(2,1)}, u32[]{:S(2)}) copy-start(bf16[512,1024]{1,0:T(8,128)(2,1)} %param.20) | copy-start | bytes 3145732
  7.2 104.9 %all-gather.6.cloned.1.call-start = ((), (), s32[]{:S(2)}) async-start(), calls=%async_computation.13 | async-start | bytes 7077888 | tf_op jit(solution)/shard_map/all_gather | solution.py:69
  8.0 554.0 %all-gather.8.cloned.1.call-start = ((), (), s32[]{:S(2)}) async-start(), calls=%async_computation.14 | async-start | bytes 2359296 | tf_op jit(solution)/shard_map/all_gather | solution.py:71
  8.7 567.8 %all-gather.10.cloned.1.call-start = ((), (), s32[]{:S(2)}) async-start(), calls=%async_computation.15 | async-start | bytes 9437184 | tf_op jit(solution)/shard_map/all_gather | solution.py:80
  67.0 51.1 %copy-start.31 = (f32[512]{0:T(512)}, f32[512]{0:T(512)S(1)}, u32[]{:S(2)}) copy-start(f32[512]{0:T(512)S(1)} %broadcast_multiply_fusion.6) | copy-start | bytes 6148
  67.5 50.7 %copy-start.33 = (f32[512]{0:T(512)}, f32[512]{0:T(512)S(1)}, u32[]{:S(2)}) copy-start(f32[512]{0:T(512)S(1)} %fusion.89) | copy-start | bytes 6148
  68.7 49.4 %copy-start.29 = (f32[1,1024]{1,0:T(1,128)}, f32[1,1024]{1,0:T(1,128)S(1)}, u32[]{:S(2)}) copy-start(f32[1,1024]{1,0:T(1,128)S(1)} %get-tuple-element.431) | copy-start | bytes 12292
  69.3 48.8 %copy-start.43 = (f32[1,1024]{1,0:T(1,128)}, f32[1,1024]{1,0:T(1,128)S(1)}, u32[]{:S(2)}) copy-start(f32[1,1024]{1,0:T(1,128)S(1)} %get-tuple-element.435) | copy-start | bytes 12292
  123.5 53.1 %all-to-all-start = ((bf16[512,3,1024]{0,1,2:T(4,128)(2,1)}), bf16[512,3,1024]{0,1,2:T(4,128)(2,1)}, u32[]{:S(2)}, u32[]{:S(2)}) async-start(bf16[512,3,1024]{0,1,2:T(4,128)(2,1)} %copy.51), calls=%async_computation | async-start | bytes 8388608 | tf_op jit(solution)/shard_map/all_to_all | solution.py:101
  128.4 460.1 %all-gather.12.cloned.1.call-start = ((), (), s32[]{:S(2)}) async-start(), calls=%async_computation.16 | async-start | bytes 9437184 | tf_op jit(solution)/shard_map/all_gather | solution.py:82
  326.7 189.4 %all-to-all-start.1 = ((bf16[4,512,256]{1,2,0:T(8,128)(2,1)}), bf16[4,512,256]{1,2,0:T(8,128)(2,1)}, u32[]{:S(2)}, u32[]{:S(2)}) async-start(bf16[4,512,256]{1,2,0:T(8,128)(2,1)} %copy.56), calls=%async_computation.1 | async-start | bytes 2097152 | tf_op jit(solution)/shard_map/all_to_all | solution.py:131
  515.0 30.8 %copy-start.49 = (bf16[2,128]{1,0:T(2,128)(2,1)S(1)}, bf16[2,128]{1,0:T(2,128)(2,1)}, u32[]{:S(2)}) copy-start(bf16[2,128]{1,0:T(2,128)(2,1)} %param.28) | copy-start | bytes 1540
  516.2 50.3 %all-to-all-start.2 = ((bf16[4,512,256]{1,2,0:T(8,128)(2,1)}), bf16[4,512,256]{1,2,0:T(8,128)(2,1)S(1)}, u32[]{:S(2)}, u32[]{:S(2)}) async-start(bf16[4,512,256]{1,2,0:T(8,128)(2,1)} %copy.59), calls=%async_computation.2 | async-start | bytes 2097152 | tf_op jit(solution)/shard_map/all_to_all | solution.py:131
  601.0 18.2 copy-start.15
  601.0 18.2 copy-start.28
  626.9 17.4 slice-start
  627.8 16.6 copy-start.8
  627.8 16.6 slice-start.1
  658.9 18.0 all-to-all-start.3
  662.4 456.4 %reduce-scatter.19.cloned.1.call-start = ((), (), s32[]{:S(2)}) async-start(), calls=%async_computation.18 | async-start | bytes 4718592 | tf_op jit(solution)/shard_map/reduce_scatter | solution.py:290
  995.0 53.2 %all-to-all-start.4 = ((bf16[2048,3,256]{2,1,0:T(4,128)(2,1)}), bf16[2048,3,256]{2,1,0:T(4,128)(2,1)}, u32[]{:S(2)}, u32[]{:S(2)}) async-start(bf16[2048,3,256]{2,1,0:T(4,128)(2,1)} %copy.64), calls=%async_computation.4 | async-start | bytes 8388608 | tf_op jit(solution)/shard_map/all_to_all | solution.py:270
  1000.0 278.3 %reduce-scatter.17.cloned.1.call-start = ((), (), s32[]{:S(2)}) async-start(), calls=%async_computation.17 | async-start | bytes 14155776 | tf_op jit(solution)/shard_map/reduce_scatter | solution.py:288
  1073.0 490.7 %reduce-scatter.21.cloned.1.call-start = ((), (), s32[]{:S(2)}) async-start(), calls=%async_computation.19 | async-start | bytes 18874368 | tf_op jit(solution)/shard_map/reduce_scatter | solution.py:291
  1085.1 764.1 %reduce-scatter.23.cloned.1.call-start = ((), (), s32[]{:S(2)}) async-start(), calls=%async_computation.20 | async-start | bytes 18874368 | tf_op jit(solution)/shard_map/reduce_scatter | solution.py:293
  1101.8 812.7 %reduce-scatter.27.cloned.1.call-start = ((), (), s32[]{:S(2)}) async-start(), calls=%async_computation.22 | async-start | bytes 589824
  1103.5 875.7 %reduce-scatter.25.cloned.1.call-start = ((), (), s32[]{:S(2)}) async-start(), calls=%async_computation.21 | async-start | bytes 589824
  1115.4 928.5 %reduce-scatter.31.cloned.1.call-start = ((), (), s32[]{:S(2)}) async-start(), calls=%async_computation.24 | async-start | bytes 589824
  1116.6 991.5 %reduce-scatter.29.cloned.1.call-start = ((), (), s32[]{:S(2)}) async-start(), calls=%async_computation.23 | async-start | bytes 589824
  1118.7 1060.8 %all-reduce.5.cloned.1.call-start = ((), (), s32[]{:S(2)}) async-start(), calls=%async_computation.25 | async-start | bytes 6291456 | tf_op jit(solution)/shard_map/psum | solution.py:299
  1851.9 63.5 %copy-start.6 = (f32[512,1024]{1,0:T(8,128)S(1)}, f32[512,1024]{1,0:T(8,128)}, u32[]{:S(2)}) copy-start(f32[512,1024]{1,0:T(8,128)} %copy-done.5) | copy-start | bytes 6291460
  (69 other events, 235.7 us)
Sparse Core Ops, SparseCore 0:
  10.2 101.8 all-gather.5
  114.3 47.4 all-gather.7
  163.9 123.3 all-gather.9
  289.3 123.6 all-gather.11
  666.6 87.0 reduce-scatter.18
  1073.2 205.0 reduce-scatter.16
  1282.5 281.1 reduce-scatter.20
  1567.5 281.6 reduce-scatter.22
  1853.5 61.0 reduce-scatter.26
  1918.3 60.9 reduce-scatter.24
  1983.0 60.9 reduce-scatter.30
  2047.1 60.9 reduce-scatter.28
  2111.4 68.0 all-reduce.4
where the time goes:
time: 2210 us; the launch traced here: 2190 us
  waiting for transfers between devices  1150 us (52%)
  matrix products  473 us (21%)
  local copies, waits for them, and re-layouts  160 us (7%)
  loops' own time  148 us (7%)
  blocking collectives  140 us (6%)
  other arithmetic  82.9 us (4%)
  starting transfers between devices  22.7 us (1%)
    reduce_scatter x1, waiting for transfers between devices, per_device(): lax.psum_scatter(grad_fc1, 'dp', scatter_dimension=0, tiled=True)  283 us
    reduce_scatter x1, waiting for transfers between devices, per_device(): lax.psum_scatter(grad_fc2, 'dp', scatter_dimension=0, tiled=True)  283 us
    unnamed x17, waiting for transfers between devices  215 us
    dot_general x68, matrix products, contract_cols(): lax.dot_general(left, right, (((1,), (1,)), ((), ())), preferred_element_...  214 us
    reduce_scatter x1, waiting for transfers between devices, per_device(): lax.psum_scatter(grad_qkv, 'dp', scatter_dimension=0, tiled=True)  158 us
    dot_general x36, matrix products, contract_rows(): lax.dot_general(left, right, (((0,), (0,)), ((), ())), preferred_element_...  92.6 us
    dot_general x32, matrix products, one_block(): out_block = jnp.dot(probs_low, v_head, preferred_element_type=jnp.float32)  87.1 us
    another operation x2, loops' own time, run_forward(): lax.map(one_block, lax.iota(jnp.int32, local_heads * blocks))  84.9 us
  transfers between devices with their start and end apart: 18, of which 12 were waited for; matrix products, arithmetic and copies ran while one was open for 28% of the time, Pallas kernels for 0%

commit v1 on v0

--- a/solution.py
+++ b/solution.py
@@ -267,7 +267,12 @@
     back_stack = jnp.stack(
         (query_grad, key_grad.astype(jnp.bfloat16), value_grad.astype(jnp.bfloat16)), axis=1
     ).reshape(seq_len, 3, local_heads * HEAD_DIM)
-    back_tokens = lax.all_to_all(back_stack, "seq", split_axis=0, concat_axis=2, tiled=True)
+    back_tokens = jnp.concatenate(
+        jax.lax.all_to_all(
+            jnp.stack(jnp.split(back_stack, jax.lax.axis_size("seq"), axis=0), axis=0), "seq", 0, 0
+        ),
+        axis=2,
+    )
     d_mixed = (
         (back_tokens.astype(jnp.float32) * scale_table())
         .astype(jnp.bfloat16)

time: 2210 us -> 2610 us (1.18)
  local copies, waits for them, and re-layouts: 160 us -> 538 us
  matrix products: 473 us -> 504 us
    dynamic_update_slice x0 -> x64, local copies, waits for them, and re-layouts: none -> 348 us  [the longest x32 174 us: back_step(): lax.dynamic_update_index_in_dim(value_grad, head_column(value_grad, head_...]
    dynamic_slice x16, local copies, waits for them, and re-layouts: 18 us -> 53.6 us  [head_column(): return lax.dynamic_index_in_dim(array, head_index, axis=1, keepdims=False)]
  transfers between devices with their start and end apart: 18 -> 18, of which waited for: 12 -> 12; matrix products, arithmetic and copies ran while one was open for 28% -> 38% of each run, Pallas kernels for 0% -> 0%
where the time goes in v1:
time: 2610 us; the launch traced here: 2590 us
  waiting for transfers between devices  1140 us (44%)
  local copies, waits for them, and re-layouts  538 us (21%)
  matrix products  504 us (19%)
  loops' own time  149 us (6%)
  blocking collectives  141 us (5%)
  other arithmetic  81.9 us (3%)
    reduce_scatter x1, waiting for transfers between devices, per_device(): lax.psum_scatter(grad_fc1, 'dp', scatter_dimension=0, tiled=True)  283 us
    reduce_scatter x1, waiting for transfers between devices, per_device(): lax.psum_scatter(grad_fc2, 'dp', scatter_dimension=0, tiled=True)  283 us
    dot_general x68, matrix products, contract_cols(): lax.dot_general(left, right, (((1,), (1,)), ((), ())), preferred_element_...  223 us
    unnamed x17, waiting for transfers between devices  215 us
    dynamic_update_slice x32, local copies, waits for them, and re-layouts, back_step(): lax.dynamic_update_index_in_dim(value_grad, head_column(value_grad, head_...  174 us
    dynamic_update_slice x32, local copies, waits for them, and re-layouts, back_step(): lax.dynamic_update_index_in_dim(key_grad, head_column(key_grad, head_inde...  174 us
    reduce_scatter x1, waiting for transfers between devices, per_device(): lax.psum_scatter(grad_qkv, 'dp', scatter_dimension=0, tiled=True)  156 us
    dot_general x36, matrix products, contract_rows(): lax.dot_general(left, right, (((0,), (0,)), ((), ())), preferred_element_...  106 us
  transfers between devices with their start and end apart: 18, of which 12 were waited for; matrix products, arithmetic and copies ran while one was open for 38% of the time, Pallas kernels for 0%

profile of v1, /device:TPU:0, one launch (start us, length us, event | category | flops | bytes accessed | tf_op | source)
XLA Modules:
  0.0 2588.3 jit_solution(14347033223160631996)
XLA Ops:
  9.5 22.3 all_gather.39
  31.8 16.7 all_gather.36
  48.5 18.3 all_gather.37
  69.3 42.9 %all-gather.6.cloned.1.call-done = bf16[1024,3072]{1,0:T(8,128)(2,1)} async-done(((bf16[128,3072]{1,0:T(8,128)(2,1)}), bf16[1024,3072]{1,0:T(8,128)(2,1)}) %all-gather.6.cloned.1.call-update) | async-done | bytes 6291472 | tf_op jit(solution)/shard_map/all_gather | solution.py:69
  129.0 47.6 %all-to-all-done = bf16[512,3,1024]{0,1,2:T(4,128)(2,1)} async-done(((bf16[512,3,1024]{0,1,2:T(4,128)(2,1)}), bf16[512,3,1024]{0,1,2:T(4,128)(2,1)}, u32[]{:S(2)}, u32[]{:S(2)}) %all-to-all-start) | async-done | bytes 3145760 | tf_op jit(solution)/shard_map/all_to_all | solution.py:101
  193.7 127.3 %while.42 = (s32[]{:T(128)}, bf16[16,512,64]{1,2,0:T(8,128)(2,1)S(1)}, s32[16]{0:T(128)S(1)}, bf16[2048,4,64]{0,2,1:T(8,128)(2,1)}, bf16[2048,4,64]{0,2,1:T(8,12...) while((s32[]{:T(128)}, ...), condition=%wide.region_5.6_spmd, body=%wide.region_2.5_spmd.sunk | while | flops 277904928 | bytes 13255076 | solution.py:125
  329.0 166.2 %while.43 = (s32[]{:T(128)}, bf16[16,512,64]{1,2,0:T(8,128)(2,1)S(1)}, f32[16,512]{1,0:T(8,128)S(1)}, s32[16]{0:T(128)S(1)}, bf16[2048,4,64]{0,2,1:T(8,128)(2,1)...) while((s32[]{:T(128)}, ...), condition=%wide.region_15.16_spmd, body=%wide.region_12.15_spmd.sunk | while | flops 277905440 | bytes 30042572 | solution.py:125
  506.6 26.0 %all-gather = bf16[8,1,512]{2,1,0:T(2,128)(2,1)S(1)} all-gather(bf16[1,1,512]{2,1,0:T(2,128)(2,1)S(1)} %reshape.353), channel_id=1, replica_groups=mesh['dp'=8,'seq'=4] {'dp'}, dimensions={0}, use_global_device_ids=true | all-gather | bytes 9216 | tf_op jit(solution)/shard_map/all_gather | solution.py:81
  532.7 16.5 all_gather.41
  563.3 11.9 fusion.97
  575.2 12.5 add_reduce_fusion
  587.7 18.2 multiply_reduce_fusion.5
  614.6 17.3 convert_reduce_fusion
  653.5 10.8 all-to-all-done.3
  671.6 732.8 %while.44 = (s32[]{:T(128)}, f32[2048,4,64]{0,1,2:T(4,128)}, f32[2048,4,64]{0,1,2:T(4,128)}, bf16[16,512,64]{1,2,0:T(8,128)(2,1)}, s32[16]{0:T(128)S(1)}, /*inde...) while((s32[]{:T(128)}, f32[2048,4,64]{0,1,2:T(4,128)}, ...), condition=%wide.region_30.31_spmd, body=%wide.region_28.30_spmd.sunk | while | flops 682917888 | bytes 74532912 | solution.py:263
  691.2 10.3 dynamic_update_slice.52
  704.9 10.3 dynamic_update_slice.53
  1071.2 10.3 dynamic_update_slice.53
  1117.0 10.3 dynamic_update_slice.53
  1208.6 10.3 dynamic_update_slice.53
  1420.7 36.8 %all-to-all-done.4 = bf16[4,512,3,256]{1,3,2,0:T(8,128)(2,1)S(1)} async-done(((bf16[4,512,3,256]{1,3,2,0:T(8,128)(2,1)}), bf16[4,512,3,256]{1,3,2,0:T(8,128)(2,1)S(1)}, u32[]{:S(2)}, u32[]{:S(2)}) %all-to-all-start.4) | async-done | bytes 3145760 | tf_op jit(solution)/shard_map/all_to_all | solution.py:271
  1469.1 13.3 fusion.96
  1482.9 15.6 fusion.98
  1518.2 155.7 %reduce-scatter.17.cloned.1.call-done = f32[128,3072]{1,0:T(8,128)} async-done(((f32[1024,3072]{1,0:T(8,128)}), f32[128,3072]{1,0:T(8,128)}) %reduce-scatter.17.cloned.1.call-update) | async-done | bytes 1572880 | tf_op jit(solution)/shard_map/reduce_scatter | solution.py:293
  1676.4 282.9 %reduce-scatter.21.cloned.1.call-done = f32[128,4096]{1,0:T(8,128)} async-done(((f32[1024,4096]{1,0:T(8,128)}), f32[128,4096]{1,0:T(8,128)}) %reduce-scatter.21.cloned.1.call-update) | async-done | bytes 2097168 | tf_op jit(solution)/shard_map/reduce_scatter | solution.py:296
  1962.0 282.9 %reduce-scatter.23.cloned.1.call-done = f32[512,1024]{1,0:T(8,128)} async-done(((f32[4096,1024]{1,0:T(8,128)}), f32[512,1024]{1,0:T(8,128)}) %reduce-scatter.23.cloned.1.call-update) | async-done | bytes 2097168 | tf_op jit(solution)/shard_map/reduce_scatter | solution.py:298
  2249.5 35.2 %all-reduce = bf16[4096]{0:T(1024)(128)(2,1)S(1)} all-reduce(f32[4096]{0:T(1024)S(1)} %copy-done.39), channel_id=6, replica_groups=mesh['dp'=8,'seq'=4] {'dp'}, use_global_device_ids=true, to_apply=%region_43.44.clone | all-reduce | flops 4096 | bytes 24576
  2284.8 25.4 reduce-scatter.27.cloned.1.call-done
  2314.4 60.5 %reduce-scatter.25.cloned.1.call-done = f32[128,2]{1,0:T(8,128)} async-done(((f32[1024,2]{1,0:T(8,128)}), f32[128,2]{1,0:T(8,128)}) %reduce-scatter.25.cloned.1.call-update) | async-done | bytes 1040
  2375.7 63.7 %reduce-scatter.31.cloned.1.call-done = f32[128,4]{1,0:T(8,128)} async-done(((f32[1024,4]{1,0:T(8,128)}), f32[128,4]{1,0:T(8,128)}) %reduce-scatter.31.cloned.1.call-update) | async-done | bytes 2064
  2440.4 63.2 %reduce-scatter.29.cloned.1.call-done = f32[128,4]{1,0:T(8,128)} async-done(((f32[1024,4]{1,0:T(8,128)}), f32[128,4]{1,0:T(8,128)}) %reduce-scatter.29.cloned.1.call-update) | async-done | bytes 2064
  2513.1 62.0 %all-reduce.5.cloned.1.call-done = (bf16[128,3072]{1,0:T(8,128)(2,1)}, bf16[128,1024]{1,0:T(8,128)(2,1)}, bf16[128,4096]{1,0:T(8,128)(2,1)}, bf16[512,1024]{1,0:T(8,128)(2,1)}) async-done(((bf16[128,3072]{1,0:T(8,128)(2,1)}, bf16[128,1024]{1,0:T(8,128)(2,1)}, bf16[128,4096]{1,0:T(8,128)(2,1)}, bf16[512,1024]{1,0:T(8,128)(2,1)}), (bf16[128,3072]{1,0:T(8,128)(2,1)}, bf16[128,1024]{1,0:T(8,128)(2,1)}, ...) | async-done | bytes 3145744 | tf_op jit(solution)/shard_map/psum | solution.py:304
  (769 shorter events, 1013.4 us)
Async XLA Ops:
  7.2 24.6 copy-start.44
  7.2 41.3 %copy-start.45 = (bf16[4,128]{1,0:T(4,128)(2,1)S(1)}, bf16[4,128]{1,0:T(4,128)(2,1)}, u32[]{:S(2)}) copy-start(bf16[4,128]{1,0:T(4,128)(2,1)} %param.30) | copy-start | bytes 3076
  7.2 59.6 %copy-start.3 = (bf16[512,1024]{1,0:T(8,128)(2,1)S(1)}, bf16[512,1024]{1,0:T(8,128)(2,1)}, u32[]{:S(2)}) copy-start(bf16[512,1024]{1,0:T(8,128)(2,1)} %param.20) | copy-start | bytes 3145732
  7.2 104.9 %all-gather.6.cloned.1.call-start = ((), (), s32[]{:S(2)}) async-start(), calls=%async_computation.13 | async-start | bytes 7077888 | tf_op jit(solution)/shard_map/all_gather | solution.py:69
  8.0 541.2 %all-gather.8.cloned.1.call-start = ((), (), s32[]{:S(2)}) async-start(), calls=%async_computation.14 | async-start | bytes 2359296 | tf_op jit(solution)/shard_map/all_gather | solution.py:71
  8.7 554.6 %all-gather.10.cloned.1.call-start = ((), (), s32[]{:S(2)}) async-start(), calls=%async_computation.15 | async-start | bytes 9437184 | tf_op jit(solution)/shard_map/all_gather | solution.py:80
  67.0 51.1 %copy-start.29 = (f32[512]{0:T(512)}, f32[512]{0:T(512)S(1)}, u32[]{:S(2)}) copy-start(f32[512]{0:T(512)S(1)} %broadcast_multiply_fusion.6) | copy-start | bytes 6148
  67.5 50.7 %copy-start.31 = (f32[512]{0:T(512)}, f32[512]{0:T(512)S(1)}, u32[]{:S(2)}) copy-start(f32[512]{0:T(512)S(1)} %fusion.87) | copy-start | bytes 6148
  68.7 49.4 %copy-start.27 = (f32[1,1024]{1,0:T(1,128)}, f32[1,1024]{1,0:T(1,128)S(1)}, u32[]{:S(2)}) copy-start(f32[1,1024]{1,0:T(1,128)S(1)} %get-tuple-element.435) | copy-start | bytes 12292
  69.3 48.8 %copy-start.42 = (f32[1,1024]{1,0:T(1,128)}, f32[1,1024]{1,0:T(1,128)S(1)}, u32[]{:S(2)}) copy-start(f32[1,1024]{1,0:T(1,128)S(1)} %get-tuple-element.439) | copy-start | bytes 12292
  123.5 53.1 %all-to-all-start = ((bf16[512,3,1024]{0,1,2:T(4,128)(2,1)}), bf16[512,3,1024]{0,1,2:T(4,128)(2,1)}, u32[]{:S(2)}, u32[]{:S(2)}) async-start(bf16[512,3,1024]{0,1,2:T(4,128)(2,1)} %copy.57), calls=%async_computation | async-start | bytes 8388608 | tf_op jit(solution)/shard_map/all_to_all | solution.py:101
  128.4 446.8 %all-gather.12.cloned.1.call-start = ((), (), s32[]{:S(2)}) async-start(), calls=%async_computation.16 | async-start | bytes 9437184 | tf_op jit(solution)/shard_map/all_gather | solution.py:82
  324.9 178.2 %all-to-all-start.1 = ((bf16[4,512,256]{1,2,0:T(8,128)(2,1)}), bf16[4,512,256]{1,2,0:T(8,128)(2,1)S(1)}, u32[]{:S(2)}, u32[]{:S(2)}) async-start(bf16[4,512,256]{1,2,0:T(8,128)(2,1)} %copy.62), calls=%async_computation.1 | async-start | bytes 2097152 | tf_op jit(solution)/shard_map/all_to_all | solution.py:131
  501.9 30.8 %copy-start.48 = (bf16[2,128]{1,0:T(2,128)(2,1)S(1)}, bf16[2,128]{1,0:T(2,128)(2,1)}, u32[]{:S(2)}) copy-start(bf16[2,128]{1,0:T(2,128)(2,1)} %param.28) | copy-start | bytes 1540
  503.1 50.3 %all-to-all-start.2 = ((bf16[4,512,256]{1,2,0:T(8,128)(2,1)}), bf16[4,512,256]{1,2,0:T(8,128)(2,1)S(1)}, u32[]{:S(2)}, u32[]{:S(2)}) async-start(bf16[4,512,256]{1,2,0:T(8,128)(2,1)} %copy.65), calls=%async_computation.2 | async-start | bytes 2097152 | tf_op jit(solution)/shard_map/all_to_all | solution.py:131
  587.7 18.3 copy-start.15
  587.7 18.3 copy-start.26
  613.7 18.1 slice-start
  614.6 17.3 copy-start.11
  614.6 17.3 slice-start.1
  646.3 18.0 all-to-all-start.3
  649.9 866.5 %reduce-scatter.19.cloned.1.call-start = ((), (), s32[]{:S(2)}) async-start(), calls=%async_computation.18 | async-start | bytes 4718592 | tf_op jit(solution)/shard_map/reduce_scatter | solution.py:295
  1416.7 40.7 %all-to-all-start.4 = ((bf16[4,512,3,256]{1,3,2,0:T(8,128)(2,1)}), bf16[4,512,3,256]{1,3,2,0:T(8,128)(2,1)S(1)}, u32[]{:S(2)}, u32[]{:S(2)}) async-start(bf16[4,512,3,256]{1,3,2,0:T(8,128)(2,1)} %pad_maximum_fusion.1), calls=%async_computation.4 | async-start | bytes 6291456 | tf_op jit(solution)/shard_map/all_to_all | solution.py:271
  1420.6 253.4 %reduce-scatter.17.cloned.1.call-start = ((), (), s32[]{:S(2)}) async-start(), calls=%async_computation.17 | async-start | bytes 14155776 | tf_op jit(solution)/shard_map/reduce_scatter | solution.py:293
  1469.1 490.2 %reduce-scatter.21.cloned.1.call-start = ((), (), s32[]{:S(2)}) async-start(), calls=%async_computation.19 | async-start | bytes 18874368 | tf_op jit(solution)/shard_map/reduce_scatter | solution.py:296
  1482.4 762.5 %reduce-scatter.23.cloned.1.call-start = ((), (), s32[]{:S(2)}) async-start(), calls=%async_computation.20 | async-start | bytes 18874368 | tf_op jit(solution)/shard_map/reduce_scatter | solution.py:298
  1498.6 811.6 %reduce-scatter.27.cloned.1.call-start = ((), (), s32[]{:S(2)}) async-start(), calls=%async_computation.22 | async-start | bytes 589824
  1500.3 874.5 %reduce-scatter.25.cloned.1.call-start = ((), (), s32[]{:S(2)}) async-start(), calls=%async_computation.21 | async-start | bytes 589824
  1511.2 928.2 %reduce-scatter.31.cloned.1.call-start = ((), (), s32[]{:S(2)}) async-start(), calls=%async_computation.24 | async-start | bytes 589824
  1512.4 991.2 %reduce-scatter.29.cloned.1.call-start = ((), (), s32[]{:S(2)}) async-start(), calls=%async_computation.23 | async-start | bytes 589824
  1516.1 1058.9 %all-reduce.5.cloned.1.call-start = ((), (), s32[]{:S(2)}) async-start(), calls=%async_computation.25 | async-start | bytes 6291456 | tf_op jit(solution)/shard_map/psum | solution.py:304
  2247.7 63.4 %copy-start.9 = (f32[512,1024]{1,0:T(8,128)S(1)}, f32[512,1024]{1,0:T(8,128)}, u32[]{:S(2)}) copy-start(f32[512,1024]{1,0:T(8,128)} %copy-done.8) | copy-start | bytes 6291460
  (83 other events, 241.9 us)
Sparse Core Ops, SparseCore 0:
  10.2 101.8 all-gather.5
  114.3 47.4 all-gather.7
  163.9 123.3 all-gather.9
  289.3 123.1 all-gather.11
  654.0 86.9 reduce-scatter.18
  1469.2 204.7 reduce-scatter.16
  1678.2 281.0 reduce-scatter.20
  1963.1 281.7 reduce-scatter.22
  2249.2 60.9 reduce-scatter.26
  2313.9 60.8 reduce-scatter.24
  2378.5 60.8 reduce-scatter.30
  2442.7 60.8 reduce-scatter.28
  2507.0 67.9 all-reduce.4
